TPU v7x, 512 devices: a whole 4x4x16 slice. The times are simulated.
512 devices in a mesh: ctx: 128 (over y_lo, x, z), head: 4 (over y_hi, core).
Axes of the slice: x: 4, y: 4 (y_hi: 2, y_lo: 2; y = y_hi * 2 + y_lo), z: 16, core: 2. Of those that a mesh axis runs over, the one named last changes fastest.
Arguments:
- hidden: bfloat16 [16384, 8192], P('ctx', 'head'), may hold values from -6 to 6
- frozen_query_rows: bfloat16 [16384, 3072], P('ctx', 'head'), may hold values from -101 to 101
- frozen_key_rows: bfloat16 [16384, 256], P('ctx'), may hold values from -5 to 5
- frozen_value_rows: bfloat16 [16384, 256], P('ctx'), may hold values from -6 to 6
- adapter_down_factors: bfloat16 [8192, 64], P('head'), may hold values from -0.0625 to 0.0625
- query_up_factor: bfloat16 [32, 3072], P(None, 'head'), may hold values from -1 to 1
- value_up_factor: bfloat16 [32, 256], replicated, may hold values from -1 to 1
- slot_span_order: int32 [256], replicated, may hold values from 0 to 255, each once
Outputs:
- attended: bfloat16 [16384, 3072], P('ctx', 'head')
- log_normalizer: float32 [24, 16384], P('head', 'ctx')
Inputs may be any that keep to these rules, and one draw needn't show every extreme that they name: `slot_span_order`: every span number appears once.
All inputs are finite; a program needn't handle non-finite values.
Results may differ from a plain program's by a relative error of at most 0.018.
Values may be sent and summed in bfloat16 or wider, within the bound.
A program may use at most 64 MiB of HBM per device.

v0:
```python
import math
import jax
import jax.numpy as jnp
from jax import lax
from jax.sharding import PartitionSpec as P

HEAD_SIZE = 128
KEY_VALUE_HEADS = 2
ADAPTER_RANK = 32
adapter_scale = 0.5
start_max = -1e30


def from_partner(value, axis, stride):
    return lax.ppermute(value, axis, [(i, i ^ 1 << stride) for i in range(lax.axis_size(axis))])


def spread_positions(span_ids, span_len):
    return (span_ids[:, None] * span_len + jnp.arange(span_len, dtype=jnp.int32)[None, :]).reshape(
        -1
    )


def stack_heads(matrix, width):
    return matrix.reshape(matrix.shape[0], -1, width).transpose(1, 0, 2).reshape(-1, width)


def empty_state(row_count, width):
    return (
        jnp.full((row_count,), start_max, jnp.float32),
        jnp.zeros((row_count,), jnp.float32),
        jnp.zeros((row_count, width), jnp.float32),
    )


def update_state(carry_state, query_matrix, query_pos, key_block, value_block, key_pos):
    running_max, denominator, numerator = carry_state
    scores = lax.dot_general(
        query_matrix, key_block, (((1,), (1,)), ((), ())), preferred_element_type=jnp.float32
    ) * (1.0 / math.sqrt(key_block.shape[1]))
    visible = key_pos[None, :] <= query_pos[:, None]
    block_max = jnp.max(jnp.where(visible, scores, -jnp.inf), axis=1)
    new_max = jnp.maximum(running_max, block_max)
    rescale = jnp.exp(running_max - new_max)
    weights = jnp.where(visible, jnp.exp(scores - new_max[:, None]), 0.0)
    denominator = denominator * rescale + jnp.sum(weights, axis=1)
    numerator = numerator * rescale[:, None] + jnp.dot(
        weights.astype(jnp.bfloat16), value_block, preferred_element_type=jnp.float32
    )
    return (new_max, denominator, numerator)


def sweep_keys(carry_state, query_matrix, query_pos, key_rows, value_rows, key_pos):
    key_count = key_rows.shape[0]
    block_len = math.gcd(key_count, 1024)

    def one_block(block_index, inner_state):
        offset = block_index * block_len
        key_block = lax.dynamic_slice_in_dim(key_rows, offset, block_len, 0)
        value_block = lax.dynamic_slice_in_dim(value_rows, offset, block_len, 0)
        pos_block = lax.dynamic_slice_in_dim(key_pos, offset, block_len, 0)
        return update_state(inner_state, query_matrix, query_pos, key_block, value_block, pos_block)

    return lax.fori_loop(0, key_count // block_len, one_block, carry_state)


def merge_states(first_state, second_state):
    first_max, first_total, first_sum = first_state
    second_max, second_total, second_sum = second_state
    new_max = jnp.maximum(first_max, second_max)
    first_scale = jnp.exp(first_max - new_max)
    second_scale = jnp.exp(second_max - new_max)
    return (
        new_max,
        first_total * first_scale + second_total * second_scale,
        first_sum * first_scale[:, None] + second_sum * second_scale[:, None],
    )


def local(
    hidden,
    frozen_query_rows,
    frozen_key_rows,
    frozen_value_rows,
    adapter_down_factors,
    query_up_factor,
    value_up_factor,
    slot_span_order,
):
    tok_dev = hidden.shape[0]
    span_len = tok_dev // 2
    partial_bottleneck = jnp.dot(hidden, adapter_down_factors, preferred_element_type=jnp.float32)
    adapter_bottleneck = lax.psum(partial_bottleneck.astype(jnp.bfloat16), "head")
    query_rows = (
        frozen_query_rows.astype(jnp.float32)
        + adapter_scale
        * jnp.dot(
            adapter_bottleneck[:, :ADAPTER_RANK],
            query_up_factor,
            preferred_element_type=jnp.float32,
        )
    ).astype(jnp.bfloat16)
    head_index = lax.axis_index("head")
    key_value_index = head_index // (lax.axis_size("head") // KEY_VALUE_HEADS)
    key_rows = lax.dynamic_slice_in_dim(frozen_key_rows, key_value_index * HEAD_SIZE, HEAD_SIZE, 1)
    value_base = lax.dynamic_slice_in_dim(
        frozen_value_rows, key_value_index * HEAD_SIZE, HEAD_SIZE, 1
    )
    value_up_update = lax.dynamic_slice_in_dim(
        value_up_factor, key_value_index * HEAD_SIZE, HEAD_SIZE, 1
    )
    value_rows = (
        value_base.astype(jnp.float32)
        + adapter_scale
        * jnp.dot(
            adapter_bottleneck[:, ADAPTER_RANK:],
            value_up_update,
            preferred_element_type=jnp.float32,
        )
    ).astype(jnp.bfloat16)
    span_pairs = slot_span_order.reshape(-1, 2)
    own_spans = lax.dynamic_slice_in_dim(span_pairs, lax.axis_index("ctx"), 1, 0).reshape(2)
    own_positions = spread_positions(own_spans, span_len)
    heads_dev = query_rows.shape[1] // HEAD_SIZE
    query_matrix = stack_heads(query_rows, HEAD_SIZE)
    query_pos = jnp.tile(own_positions, heads_dev)
    own_count = query_matrix.shape[0]
    half_side = head_index % 2
    partner = from_partner(query_matrix, "head", 0)
    stacked = jnp.concatenate([query_matrix, partner], axis=0)
    stacked_pos = jnp.concatenate([query_pos, query_pos])
    key_half = lax.dynamic_slice_in_dim(key_rows, half_side * span_len, span_len, 0)
    value_half = lax.dynamic_slice_in_dim(value_rows, half_side * span_len, span_len, 0)
    span_ids = jnp.where(half_side == 0, span_pairs[:, 0], span_pairs[:, 1])
    running_max, denominator, numerator = sweep_keys(
        empty_state(2 * own_count, HEAD_SIZE),
        stacked,
        stacked_pos,
        lax.all_gather(key_half, "ctx", axis=0, tiled=True),
        lax.all_gather(value_half, "ctx", axis=0, tiled=True),
        spread_positions(span_ids, span_len),
    )
    returned = (
        from_partner(running_max[own_count:].astype(jnp.bfloat16), "head", 0).astype(jnp.float32),
        from_partner(denominator[own_count:].astype(jnp.bfloat16), "head", 0).astype(jnp.float32),
        from_partner(numerator[own_count:].astype(jnp.bfloat16), "head", 0).astype(jnp.float32),
    )
    running_max, denominator, numerator = merge_states(
        (running_max[:own_count], denominator[:own_count], numerator[:own_count]), returned
    )
    result = (numerator / denominator[:, None]).astype(jnp.bfloat16)
    attended = (
        result.reshape(heads_dev, tok_dev, HEAD_SIZE)
        .transpose(1, 0, 2)
        .reshape(tok_dev, heads_dev * HEAD_SIZE)
    )
    log_normalizer = (running_max + jnp.log(denominator)).reshape(heads_dev, tok_dev)
    return (attended, log_normalizer)


def solution(mesh):
    placed = (
        P("ctx", "head"),
        P("ctx", "head"),
        P("ctx", None),
        P("ctx", None),
        P("head", None),
        P(None, "head"),
        P(),
        P(),
    )
    return jax.shard_map(
        local,
        mesh=mesh,
        in_specs=placed,
        out_specs=(P("ctx", "head"), P("head", "ctx")),
        check_vma=False,
    )
```

profile of v0, /device:TPU:1, one launch (start us, length us, event | category | flops | bytes accessed | tf_op | source)
XLA Modules:
  0.0 1264.8 jit_solution(4207218404230548502)
XLA Ops:
  7.3 1.5 dynamic_slice.38
  8.9 1.3 convolution_convert_fusion
  10.1 16.1 %psum.7 = bf16[128,64]{0,1:T(8,128)(2,1)S(1)} all-reduce(bf16[128,64]{0,1:T(8,128)(2,1)S(1)} %convolution_convert_fusion), channel_id=1, replica_groups=mesh['ctx'=128,'head'=4] {'head'}, use_global_device_ids=true, to_apply=%region_0.0 | all-reduce | flops 8192 | bytes 32768 | tf_op jit(solution)/shard_map/psum | solution.py:93
  26.3 0.9 fusion.24
  27.1 1.3 fusion.23
  28.5 1.2 fusion.19
  29.7 0.2 copy.14
  29.9 0.2 copy.15
  30.0 5.7 collective-permute-start
  35.8 0.8 reshape.57
  36.7 0.1 add.124
  36.8 0.2 fusion.21
  37.0 0.1 iota_add_fusion
  37.2 477.1 %all-gather.3.cloned.1.call-done = bf16[8192,128]{1,0:T(8,128)(2,1)} async-done(((bf16[64,128]{1,0:T(8,128)(2,1)}), bf16[8192,128]{1,0:T(8,128)(2,1)}) %all-gather.3.cloned.1.call-update) | async-done | bytes 2097168 | tf_op jit(solution)/shard_map/all_gather | solution.py:139
  514.4 585.6 %all-gather.5.cloned.1.call-done = bf16[8192,128]{1,0:T(8,128)(2,1)} async-done(((bf16[64,128]{1,0:T(8,128)(2,1)}), bf16[8192,128]{1,0:T(8,128)(2,1)}) %all-gather.5.cloned.1.call-update) | async-done | bytes 2097168 | tf_op jit(solution)/shard_map/all_gather | solution.py:140
  1099.9 55.1 %while.18 = (s32[]{:T(128)}, f32[1536]{0:T(1024)S(1)}, f32[1536]{0:T(1024)S(1)}, f32[1536,128]{1,0:T(8,128)S(1)}, s32[8192]{0:T(1024)S(1)}, /*index=5*/s32[1536]...) while((s32[]{:T(128)}, f32[1536]{0:T(1024)S(1)}, ...), condition=%wide.region_4.5_spmd.clone, body=%wide.region_1.4_spmd.clone.sunk | while | flops 827923968 | bytes 21502156 | solution.py:64
  1099.9 1.9 fusion.52
  1101.9 1.9 fusion.53
  1103.8 2.9 fusion.55
  1106.8 2.0 fusion.52
  1108.8 1.9 fusion.53
  1110.7 2.9 fusion.55
  1113.7 2.0 fusion.52
  1115.7 1.9 fusion.53
  1117.6 2.9 fusion.55
  1120.6 2.0 fusion.52
  1122.6 1.9 fusion.53
  1124.5 2.9 fusion.55
  1127.5 2.0 fusion.52
  1129.5 1.9 fusion.53
  1131.4 2.9 fusion.55
  1134.4 2.0 fusion.52
  1136.4 1.9 fusion.53
  1138.3 2.9 fusion.55
  1141.3 2.0 fusion.52
  1143.2 1.9 fusion.53
  1145.2 2.9 fusion.55
  1148.1 2.0 fusion.52
  1150.1 1.9 fusion.53
  1152.0 2.9 fusion.55
  1155.0 96.1 %collective-permute-start.3 = (bf16[768]{0:T(1024)(128)(2,1)S(1)}, bf16[768]{0:T(1024)(128)(2,1)S(1)}, u32[]{:S(2)}, u32[]{:S(2)}) collective-permute-start(bf16[768]{0:T(1024)(128)(2,1)S(1)} %slice.69), channel_id=1, source_target_pairs={{0,1},{1,0},{2,3},{3,2},{4,5},{5,4},{6,7},{7,6},{8,9},{9,8},{10,11... | collective-permute-start | bytes 4616 | tf_op jit(solution)/shard_map/ppermute | solution.py:15
  1251.2 1.9 collective-permute-start.1
  1253.1 2.4 collective-permute-start.2
  1255.5 0.6 fusion.31
  1256.2 0.4 collective-permute-done.2
  1256.6 0.4 divide_convert_fusion
  1256.9 0.2 copy.16
  1257.1 0.8 copy.17
  (53 shorter events, 0.6 us)
Async XLA Ops:
  7.2 1.7 copy-start
  7.2 507.2 %all-gather.3.cloned.1.call-start = ((), (), s32[]{:S(2)}) async-start(), calls=%async_computation | async-start | bytes 2113536 | tf_op jit(solution)/shard_map/all_gather | solution.py:139
  8.8 1091.1 %all-gather.5.cloned.1.call-start = ((), (), s32[]{:S(2)}) async-start(), calls=%async_computation.1 | async-start | bytes 2113536 | tf_op jit(solution)/shard_map/all_gather | solution.py:140
  30.0 7.2 collective-permute-start
  1155.0 100.5 %collective-permute-start.3 = (bf16[768]{0:T(1024)(128)(2,1)S(1)}, bf16[768]{0:T(1024)(128)(2,1)S(1)}, u32[]{:S(2)}, u32[]{:S(2)}) collective-permute-start(bf16[768]{0:T(1024)(128)(2,1)S(1)} %slice.69), channel_id=1, source_target_pairs={{0,1},{1,0},{2,3},{3,2},{4,5},{5,4},{6,7},{7,6},{8,9},{9,8},{10,11... | collective-permute-start | bytes 4616 | tf_op jit(solution)/shard_map/ppermute | solution.py:15
  1251.2 4.4 collective-permute-start.1
  1253.1 3.5 collective-permute-start.2
Sparse Core Ops, SparseCore 0:
  10.6 503.6 all-gather.2
  516.4 583.4 all-gather.4
where the time goes:
time: 1270 us; the launch traced here: 1260 us
  waiting for transfers between devices  1060 us (83%)
  starting transfers between devices  106 us (8%)
  matrix products  42.5 us (3%)
  other arithmetic  17.9 us (1%)
  blocking collectives  16.1 us (1%)
  between operations  14.3 us (1%)
    all_gather x1, waiting for transfers between devices, local(): lax.all_gather(value_half, 'ctx', axis=0, tiled=True)  586 us
    all_gather x1, waiting for transfers between devices, local(): lax.all_gather(key_half, 'ctx', axis=0, tiled=True)  477 us
    ppermute x4, starting transfers between devices, from_partner(): lax.ppermute(value, axis, [(i, i ^ 1 << stride) for i in range(lax.axis_s...  106 us
  transfers between devices with their start and end apart: 6, of which 3 were waited for; matrix products, arithmetic and copies ran while one was open for 1% of the time, Pallas kernels for 0%

commit v1 on v0

--- a/solution.py
+++ b/solution.py
@@ -136,7 +136,9 @@
         empty_state(2 * own_count, HEAD_SIZE),
         stacked,
         stacked_pos,
-        lax.all_gather(key_half, "ctx", axis=0, tiled=True),
+        jnp.concatenate(
+            lax.all_to_all(jnp.stack([key_half] * lax.axis_size("ctx")), "ctx", 0, 0), axis=0
+        ),
         lax.all_gather(value_half, "ctx", axis=0, tiled=True),
         spread_positions(span_ids, span_len),
     )

time: 1270 us -> 719 us (0.57)
  waiting for transfers between devices: 1060 us -> 501 us
  starting transfers between devices: 106 us -> 126 us
    all_gather x1 -> x0, waiting for transfers between devices: 477 us -> none  [local(): lax.all_gather(key_half, 'ctx', axis=0, tiled=True)]
    all_gather x1, waiting for transfers between devices: 586 us -> 500 us  [local(): lax.all_gather(value_half, 'ctx', axis=0, tiled=True)]
    all_to_all x0 -> x1, starting transfers between devices: none -> 21.3 us  [local(): lax.all_to_all(jnp.stack([key_half] * lax.axis_size('ctx')), 'ctx', 0, 0)]
where the time goes in v1:
time: 719 us; the launch traced here: 718 us
  waiting for transfers between devices  501 us (70%)
  starting transfers between devices  126 us (18%)
  matrix products  32.3 us (4%)
  other arithmetic  18.9 us (3%)
  between operations  14.3 us (2%)
  blocking collectives  13.4 us (2%)
  local copies, waits for them, and re-layouts  12.5 us (2%)
    all_gather x1, waiting for transfers between devices, local(): lax.all_gather(value_half, 'ctx', axis=0, tiled=True)  500 us
    ppermute x4, starting transfers between devices, from_partner(): lax.ppermute(value, axis, [(i, i ^ 1 << stride) for i in range(lax.axis_s...  104 us
    dot_general x8, matrix products, update_state(): jnp.dot(weights.astype(jnp.bfloat16), value_block, preferred_element_type...  23.5 us
    all_to_all x1, starting transfers between devices, local(): lax.all_to_all(jnp.stack([key_half] * lax.axis_size('ctx')), 'ctx', 0, 0)  21.3 us
    reduce_sum x8, other arithmetic, update_state(): denominator = denominator * rescale + jnp.sum(weights, axis=1)  15 us
  transfers between devices with their start and end apart: 6, of which 3 were waited for; matrix products, arithmetic and copies ran while one was open for 1% of the time, Pallas kernels for 0%

profile of v1, /device:TPU:1, one launch (start us, length us, event | category | flops | bytes accessed | tf_op | source)
XLA Modules:
  0.0 718.0 jit_solution(5876102946501772765)
XLA Ops:
  7.3 0.9 dynamic_slice.38
  8.2 1.8 stack.2
  10.0 21.3 %all-to-all-start = ((bf16[128,64,128]{2,1,0:T(8,128)(2,1)}), bf16[128,64,128]{2,1,0:T(8,128)(2,1)S(1)}, u32[]{:S(2)}, u32[]{:S(2)}) async-start(bf16[128,64,128]{2,1,0:T(8,128)(2,1)} %stack.2), calls=%async_computation | async-start | bytes 4194304 | tf_op jit(solution)/shard_map/all_to_all | solution.py:140
  31.8 13.4 %psum.7 = bf16[128,64]{0,1:T(8,128)(2,1)S(1)} all-reduce(bf16[128,64]{0,1:T(8,128)(2,1)S(1)} %convolution_convert_fusion), channel_id=1, replica_groups=mesh['ctx'=128,'head'=4] {'head'}, use_global_device_ids=true, to_apply=%region_0.0 | all-reduce | flops 8192 | bytes 32768 | tf_op jit(solution)/shard_map/psum | solution.py:93
  45.3 1.3 fusion.23
  47.3 5.1 collective-permute-start
  53.5 499.8 %all-gather.2.cloned.1.call-done = bf16[8192,128]{1,0:T(8,128)(2,1)} async-done(((bf16[64,128]{1,0:T(8,128)(2,1)}), bf16[8192,128]{1,0:T(8,128)(2,1)}) %all-gather.2.cloned.1.call-update) | async-done | bytes 2097168 | tf_op jit(solution)/shard_map/all_gather | solution.py:142
  553.3 54.3 %while.18 = (s32[]{:T(128)}, f32[1536]{0:T(1024)S(1)}, f32[1536]{0:T(1024)S(1)}, f32[1536,128]{1,0:T(8,128)}, s32[8192]{0:T(1024)S(1)}, /*index=5*/s32[1536]{0:T...) while((s32[]{:T(128)}, f32[1536]{0:T(1024)S(1)}, ...), condition=%wide.region_4.5_spmd.clone, body=%wide.region_1.4_spmd.clone.sunk | while | flops 827923968 | bytes 27795716 | solution.py:64
  553.3 1.0 fusion.52
  554.3 1.9 fusion.53
  556.2 2.9 fusion.55
  559.2 0.9 copy-done.2
  560.0 1.0 fusion.52
  561.1 1.9 fusion.53
  563.0 2.9 fusion.55
  566.0 0.9 copy-done.2
  566.8 1.0 fusion.52
  567.9 1.9 fusion.53
  569.8 2.9 fusion.55
  572.8 0.9 copy-done.2
  573.6 1.0 fusion.52
  574.7 1.9 fusion.53
  576.6 2.9 fusion.55
  579.5 0.9 copy-done.2
  580.4 1.0 fusion.52
  581.5 1.9 fusion.53
  583.4 2.9 fusion.55
  586.3 0.9 copy-done.2
  587.2 1.0 fusion.52
  588.2 1.9 fusion.53
  590.2 2.9 fusion.55
  593.1 0.9 copy-done.2
  594.0 1.0 fusion.52
  595.0 1.9 fusion.53
  596.9 2.9 fusion.55
  599.9 0.9 copy-done.2
  600.8 1.0 fusion.52
  601.8 1.9 fusion.53
  603.7 2.9 fusion.55
  606.7 0.9 copy-done.2
  607.6 94.8 %collective-permute-start.3 = (bf16[768]{0:T(1024)(128)(2,1)S(1)}, bf16[768]{0:T(1024)(128)(2,1)S(1)}, u32[]{:S(2)}, u32[]{:S(2)}) collective-permute-start(bf16[768]{0:T(1024)(128)(2,1)S(1)} %slice.69), channel_id=1, source_target_pairs={{0,1},{1,0},{2,3},{3,2},{4,5},{5,4},{6,7},{7,6},{8,9},{9,8},{10,11... | collective-permute-start | bytes 4616 | tf_op jit(solution)/shard_map/ppermute | solution.py:15
  702.4 1.9 collective-permute-start.1
  704.3 1.0 slice.68
  705.3 2.4 collective-permute-start.2
  707.8 0.6 fusion.31
  708.4 0.4 collective-permute-done.2
  708.8 1.4 divide_convert_fusion
  710.3 0.8 copy.17
  (95 shorter events, 2.6 us)
Async XLA Ops:
  7.2 24.3 %copy-start = (bf16[128,2048]{1,0:T(8,128)(2,1)S(1)}, bf16[128,2048]{1,0:T(8,128)(2,1)}, u32[]{:S(2)}) copy-start(bf16[128,2048]{1,0:T(8,128)(2,1)} %param.10) | copy-start | bytes 1572868
  7.2 24.2 %copy-start.3 = (bf16[2048,64]{0,1:T(8,128)(2,1)S(1)}, bf16[2048,64]{0,1:T(8,128)(2,1)}, u32[]{:S(2)}) copy-start(bf16[2048,64]{0,1:T(8,128)(2,1)} %param.14) | copy-start | bytes 786436
  7.2 38.0 %copy-start.6 = (bf16[32,256]{1,0:T(8,128)(2,1)S(1)}, bf16[32,256]{1,0:T(8,128)(2,1)}, u32[]{:S(2)}) copy-start(bf16[32,256]{1,0:T(8,128)(2,1)} %param.16) | copy-start | bytes 49156
  7.2 39.5 %copy-start.5 = (bf16[32,768]{1,0:T(8,128)(2,1)S(1)}, bf16[32,768]{1,0:T(8,128)(2,1)}, u32[]{:S(2)}) copy-start(bf16[32,768]{1,0:T(8,128)(2,1)} %param.15) | copy-start | bytes 147460
  7.2 39.5 %copy-start.4 = (bf16[128,768]{1,0:T(8,128)(2,1)S(1)}, bf16[128,768]{1,0:T(8,128)(2,1)}, u32[]{:S(2)}) copy-start(bf16[128,768]{1,0:T(8,128)(2,1)} %param.11) | copy-start | bytes 589828
  7.2 45.2 %copy-start.7 = (s32[256]{0:T(256)S(1)}, s32[256]{0:T(256)}, u32[]{:S(2)}) copy-start(s32[256]{0:T(256)} %param.17) | copy-start | bytes 3076
  10.0 543.2 %all-to-all-start = ((bf16[128,64,128]{2,1,0:T(8,128)(2,1)}), bf16[128,64,128]{2,1,0:T(8,128)(2,1)S(1)}, u32[]{:S(2)}, u32[]{:S(2)}) async-start(bf16[128,64,128]{2,1,0:T(8,128)(2,1)} %stack.2), calls=%async_computation | async-start | bytes 4194304 | tf_op jit(solution)/shard_map/all_to_all | solution.py:140
  31.4 521.9 %all-gather.2.cloned.1.call-start = ((), (), s32[]{:S(2)}) async-start(), calls=%async_computation.1 | async-start | bytes 2113536 | tf_op jit(solution)/shard_map/all_gather | solution.py:142
  47.3 6.1 collective-permute-start
  554.3 1.9 copy-start.1
  559.2 0.9 copy-start.2
  561.1 1.9 copy-start.1
  565.9 0.9 copy-start.2
  567.9 1.9 copy-start.1
  572.7 0.9 copy-start.2
  574.6 1.9 copy-start.1
  579.5 0.9 copy-start.2
  581.4 1.9 copy-start.1
  586.3 0.9 copy-start.2
  588.2 1.9 copy-start.1
  593.1 0.9 copy-start.2
  595.0 1.9 copy-start.1
  599.9 0.9 copy-start.2
  601.8 1.9 copy-start.1
  606.7 0.9 copy-start.2
  607.6 100.2 %collective-permute-start.3 = (bf16[768]{0:T(1024)(128)(2,1)S(1)}, bf16[768]{0:T(1024)(128)(2,1)S(1)}, u32[]{:S(2)}, u32[]{:S(2)}) collective-permute-start(bf16[768]{0:T(1024)(128)(2,1)S(1)} %slice.69), channel_id=1, source_target_pairs={{0,1},{1,0},{2,3},{3,2},{4,5},{5,4},{6,7},{7,6},{8,9},{9,8},{10,11... | collective-permute-start | bytes 4616 | tf_op jit(solution)/shard_map/ppermute | solution.py:15
  702.4 5.4 collective-permute-start.1
  705.3 3.5 collective-permute-start.2
Sparse Core Ops, SparseCore 0:
  46.8 506.3 all-gather.1
